TPU v7x, 128 devices: a whole 4x4x4 slice. The times are simulated.
128 devices in a mesh: gx: 8 (over x, core), gy: 4 (over z), band: 4 (over y).
Axes of the slice: x: 4, y: 4, z: 4, core: 2. Of those that a mesh axis runs over, the one named last changes fastest.
Arguments:
- block: float32 [32, 96, 18432], P('band', 'gx', 'gy'), may hold values from -9 to 9
- prior: float32 [256, 96, 18432], P('band', 'gx', 'gy'), may hold values from -9 to 9
- potential: float32 [96, 18432], P('gx', 'gy'), may hold values from -1.5 to 1
Outputs:
- orbitals: float32 [32, 96, 18432], P('band', 'gx', 'gy')
All inputs are finite; a program needn't handle non-finite values.
Results may differ from a plain program's by a relative error of at most 0.000098.
Values sent between devices are 32-bit elements; how exact they have to be, the bound alone decides.
A program may use at most 128 MiB of HBM per device.

v0:
```python
import jax
import jax.numpy as jnp
from jax import lax
from jax.sharding import PartitionSpec as P

NZ = 192
coeffs = (-205.0 / 72.0, 8.0 / 5.0, -1.0 / 5.0, 8.0 / 315.0, -1.0 / 560.0)


def extended_2(x, sides, width):
    for axis, dim in sides:
        devices, length = (lax.axis_size(axis), x.shape[dim])
        up = [(i, (i + 1) % devices) for i in range(devices - 1)]
        down = [(j, i) for i, j in up]
        last = lax.slice_in_dim(x, length - width, length, axis=dim)
        leading = lax.slice_in_dim(x, 0, width, axis=dim)
        before = lax.ppermute(last, axis, up)
        after = lax.ppermute(leading, axis, down)
        x = jnp.concatenate([before, x, after], axis=dim)
    return x


def laplace(padded):
    center = padded[:, 4:-4, 4:-4, 4:-4]
    total = 3.0 * coeffs[0] * center
    for shift in range(1, 5):
        total = total + coeffs[shift] * (
            padded[:, 4 + shift : padded.shape[1] - 4 + shift, 4:-4, 4:-4]
            + padded[:, 4 - shift : padded.shape[1] - 4 - shift, 4:-4, 4:-4]
        )
        total = total + coeffs[shift] * (
            padded[:, 4:-4, 4 + shift : padded.shape[2] - 4 + shift, 4:-4]
            + padded[:, 4:-4, 4 - shift : padded.shape[2] - 4 - shift, 4:-4]
        )
        total = total + coeffs[shift] * (
            padded[:, 4:-4, 4:-4, 4 + shift : padded.shape[3] - 4 + shift]
            + padded[:, 4:-4, 4:-4, 4 - shift : padded.shape[3] - 4 - shift]
        )
    return total


def matmul(left, right):
    return jnp.dot(left, right, precision=lax.Precision.HIGHEST, preferred_element_type=jnp.float32)


def shards(block, prior, potential):
    own_count = block.shape[0]
    rows_x = block.shape[1]
    rows_y = block.shape[2] // NZ
    total_count = own_count * lax.axis_size("band")
    ncells_all = rows_x * lax.axis_size("gx") * rows_y * lax.axis_size("gy") * NZ
    grid_block = block.reshape(own_count, rows_x, rows_y, NZ)
    extended = extended_2(grid_block, (("gx", 1), ("gy", 2)), 4)
    extended = jnp.pad(extended, ((0, 0), (0, 0), (0, 0), (4, 4)))
    lap_flat = laplace(extended).reshape(block.shape)
    phi = -2.0 * lap_flat + potential[None] * block
    phi_flat = phi.reshape(own_count, -1)
    prior_flat = prior.reshape(prior.shape[0], -1)
    phi_all = lax.all_gather(phi_flat, "band", axis=0, tiled=True)
    correlation = lax.psum(matmul(prior_flat, phi_all.T), ("gx", "gy")) / ncells_all
    removed = lax.psum_scatter(
        matmul(correlation.T, prior_flat), "band", scatter_dimension=0, tiled=True
    )
    projected_own = phi_flat - removed
    projected = lax.all_gather(projected_own, "band", axis=0, tiled=True)
    gram = lax.psum(matmul(projected, projected.T), ("gx", "gy")) / ncells_all
    lower = jnp.linalg.cholesky(gram)
    inverse = lax.linalg.triangular_solve(
        lower, jnp.eye(total_count, dtype=lower.dtype), left_side=True, lower=True
    )
    first_row = lax.axis_index("band") * own_count
    own_rows = lax.dynamic_slice_in_dim(inverse, first_row, own_count, 0)
    orbitals = matmul(own_rows, projected)
    return orbitals.reshape(block.shape)


def solution(mesh):
    in_specs = (P("band", "gx", "gy"), P("band", "gx", "gy"), P("gx", "gy"))
    out_specs = P("band", "gx", "gy")
    return jax.shard_map(shards, mesh=mesh, in_specs=in_specs, out_specs=out_specs, check_vma=False)
```

profile of v0, /device:TPU:0, one launch (start us, length us, event | category | flops | bytes accessed | tf_op | source)
XLA Modules:
  0.0 602.9 jit_solution(7956143481172874915)
XLA Ops:
  6.5 0.0 all-gather.3.cloned.1.call-start
  6.5 2.0 reshape.25
  8.5 0.0 copy-start.2
  8.5 0.1 fusion.48
  8.7 1.3 collective-permute-start.1
  10.0 1.3 collective-permute-start
  11.3 0.5 collective-permute-done.1
  11.9 0.1 constant_dynamic-update-slice_fusion.3
  12.0 0.0 copy-done.2
  12.0 0.8 constant_dynamic-update-slice_fusion.1
  12.9 0.0 copy-start.1
  12.9 3.1 collective-permute-done
  16.0 0.1 constant_dynamic-update-slice_fusion
  16.1 0.0 copy-start
  16.1 0.0 copy-start.3
  16.1 0.3 fusion.47
  16.4 0.0 copy-done.1
  16.4 1.3 collective-permute-start.2
  17.7 4.6 collective-permute-start.3
  22.3 6.6 %collective-permute-done.2 = f32[8,20,4,192]{3,2,0,1:T(4,128)S(1)} collective-permute-done((f32[8,20,4,192]{3,2,0,1:T(4,128)S(1)}, f32[8,20,4,192]{3,2,0,1:T(4,128)S(1)}, u32[]{:S(2)}, u32[]{:S(2)}) %collective-permute-start.2) | collective-permute-done | bytes 491552 | tf_op jit(solution)/shard_map/ppermute | solution.py:18
  28.9 1.5 collective-permute-done.3
  30.3 2.9 select_maximum_fusion
  33.2 0.0 copy-done
  33.2 0.0 copy-done.3
  33.2 20.7 %fusion.9 = f32[8,12,24,192]{3,2,0,1:T(8,128)} fusion(f32[8,20,24,192]{3,2,0,1:T(8,128)} %copy-done.3, f32[8,20,4,192]{3,2,0,1:T(4,128)S(1)} %collective-permute-done.3, f32[8,20,4,192]{3,2,0,1:T(4,128)S(1)} %collective-permute-done.2, f32[8,20,32,200]{3,2,0,1:T(8,128)S(1)} %select_maximum_fusion, f32[8,16,24,192]{3,2,0,1:T(8,128)} %copy-done.1, ...), kind=kLoop, calls=%fused_computation.25 | loop fusion | flops 20348928 | bytes 35782656 | tf_op jit(solution)/shard_map/mul | solution.py:56
  53.9 0.0 copy-start.5
  53.9 2.3 mul.78
  56.2 0.0 copy-done.5
  56.2 2.4 multiply_add_fusion
  58.6 0.0 all-gather.3.cloned.1.call-update
  58.7 0.2 reduce-scatter.2.cloned.1.call-start
  58.9 11.4 %copy.10 = f32[12,8,8,4608]{3,2,0,1:T(8,128)} copy(f32[12,8,8,4608]{3,2,1,0:T(8,128)} %bitcast.31) | data formatting | bytes 28311552 | tf_op jit(solution)/shard_map/reshape | solution.py:58
  70.3 79.2 %all-gather.3.cloned.1.call-done = f32[32,55296]{1,0:T(8,128)} async-done(((f32[8,55296]{1,0:T(8,128)}), f32[32,55296]{1,0:T(8,128)}) %all-gather.3.cloned.1.call-update) | async-done | bytes 7077904 | tf_op jit(solution)/shard_map/all_gather | solution.py:59
  149.5 14.5 %convolution_bitcast_fusion = f32[64,32]{0,1:T(8,128)S(1)} fusion(f32[32,55296]{1,0:T(8,128)} %all-gather.3.cloned.1.call-done, f32[64,55296]{1,0:T(8,128)} %bitcast.27), kind=kOutput, calls=%fused_computation.63 | convolution fusion | flops 1358954496 | bytes 21241856 | tf_op jit(solution)/shard_map/dot_general | solution.py:43
  164.0 128.3 %psum.14 = f32[64,32]{0,1:T(8,128)S(1)} all-reduce(f32[64,32]{0,1:T(8,128)S(1)} %convolution_bitcast_fusion), channel_id=1, replica_groups=mesh['gx'=8,'gy'=4,'band'=4] {'gx','gy'}, use_global_device_ids=true, to_apply=%region_0.1 | all-reduce | flops 2048 | bytes 16384 | tf_op jit(solution)/shard_map/psum | solution.py:60
  292.3 11.7 %fusion.40 = f32[32,55296]{1,0:T(8,128)} fusion(f32[64,55296]{1,0:T(8,128)} %bitcast.28, f32[64,32]{0,1:T(8,128)S(1)} %psum.14), kind=kOutput, calls=%fused_computation.78 | convolution fusion | flops 1358956544 | bytes 21241856 | tf_op jit(solution)/shard_map/dot_general | solution.py:43
  304.0 0.0 copy-start.4
  304.0 0.0 reduce-scatter.2.cloned.1.call-update
  304.0 0.0 all-gather.5.cloned.1.call-start
  304.0 66.2 %reduce-scatter.2.cloned.1.call-done = f32[8,55296]{1,0:T(8,128)} async-done(((f32[32,55296]{1,0:T(8,128)}), f32[8,55296]{1,0:T(8,128)}) %reduce-scatter.2.cloned.1.call-update) | async-done | bytes 1769488 | tf_op jit(solution)/shard_map/reduce_scatter | solution.py:61
  370.3 0.0 copy-done.4
  370.3 2.9 sub.3
  373.1 0.0 all-gather.5.cloned.1.call-update
  373.1 72.1 %all-gather.5.cloned.1.call-done = f32[32,55296]{1,0:T(8,128)} async-done(((f32[8,55296]{1,0:T(8,128)}), f32[32,55296]{1,0:T(8,128)}) %all-gather.5.cloned.1.call-update) | async-done | bytes 7077904 | tf_op jit(solution)/shard_map/all_gather | solution.py:65
  445.3 9.1 %fusion.49 = f32[32,32]{0,1:T(8,128)S(1)} fusion(f32[32,55296]{1,0:T(8,128)} %all-gather.5.cloned.1.call-done), kind=kOutput, calls=%fused_computation.91 | convolution fusion | flops 679477248 | bytes 7081984 | tf_op jit(solution)/shard_map/dot_general | solution.py:43
  454.4 128.5 %psum.15 = f32[32,32]{0,1:T(8,128)S(1)} all-reduce(f32[32,32]{0,1:T(8,128)S(1)} %fusion.49), channel_id=1, replica_groups=mesh['gx'=8,'gy'=4,'band'=4] {'gx','gy'}, use_global_device_ids=true, to_apply=%region_2.3 | all-reduce | flops 1024 | bytes 8192 | tf_op jit(solution)/shard_map/psum | solution.py:66
  582.9 0.1 copy.8
  583.0 2.9 cholesky.17
  585.9 0.6 compare_reduce_fusion
  586.6 0.7 fusion.36
  587.2 2.4 custom-call.6
  589.6 0.2 fusion.37
  589.9 6.5 %fusion.43 = f32[8,55296]{1,0:T(8,128)} fusion(f32[32,55296]{1,0:T(8,128)} %all-gather.5.cloned.1.call-done, f32[32,32]{1,0:T(8,128)S(1)} %fusion.37, s32[]{:T(128)S(6)} %select_n.8), kind=kOutput, calls=%fused_computation.84 | convolution fusion | flops 169869312 | bytes 8851460 | tf_op jit(solution)/shard_map/dot_general | solution.py:43
  (3 shorter events, 0.0 us)
Async XLA Ops:
  6.5 142.9 %all-gather.3.cloned.1.call-start = ((), (), s32[]{:S(2)}) async-start(), calls=%async_computation.1 | async-start | bytes 8847360 | tf_op jit(solution)/shard_map/all_gather | solution.py:59
  8.5 3.5 copy-start.2
  8.7 3.2 collective-permute-start.1
  10.0 5.9 collective-permute-start
  12.9 3.5 copy-start.1
  16.1 17.1 %copy-start = (f32[8,16,24,192]{3,2,0,1:T(8,128)}, f32[8,16,24,192]{3,2,0,1:T(8,128)S(1)}, u32[]{:S(2)}) copy-start(f32[8,16,24,192]{3,2,0,1:T(8,128)S(1)} %get-tuple-element.12) | copy-start | bytes 7077892
  16.1 17.1 %copy-start.3 = (f32[8,20,24,192]{3,2,0,1:T(8,128)}, f32[8,20,24,192]{3,2,0,1:T(8,128)S(1)}, u32[]{:S(2)}) copy-start(f32[8,20,24,192]{3,2,0,1:T(8,128)S(1)} %get-tuple-element.13) | copy-start | bytes 8847364
  16.4 12.5 %collective-permute-start.2 = (f32[8,20,4,192]{3,2,0,1:T(4,128)S(1)}, f32[8,20,4,192]{3,2,0,1:T(4,128)S(1)}, u32[]{:S(2)}, u32[]{:S(2)}) collective-permute-start(f32[8,20,4,192]{3,2,0,1:T(4,128)S(1)} %get-tuple-element.5), channel_id=1, source_target_pairs={{4,0},{8,4},{12,8},{5,1},{9,5},{13,9},{6,2},{10,6},{14,10},{7,3},{... | collective-permute-start | bytes 1474568 | tf_op jit(solution)/shard_map/ppermute | solution.py:18
  17.7 12.6 %collective-permute-start.3 = (f32[8,20,4,192]{3,2,0,1:T(4,128)S(1)}, f32[8,20,4,192]{3,2,0,1:T(4,128)S(1)}, u32[]{:S(2)}, u32[]{:S(2)}) collective-permute-start(f32[8,20,4,192]{3,2,0,1:T(4,128)S(1)} %get-tuple-element.6), channel_id=1, source_target_pairs={{0,4},{4,8},{8,12},{1,5},{5,9},{9,13},{2,6},{6,10},{10,14},{3,7},{... | collective-permute-start | bytes 1474568 | tf_op jit(solution)/shard_map/ppermute | solution.py:17
  53.9 2.3 copy-start.5
  58.7 311.6 %reduce-scatter.2.cloned.1.call-start = ((), (), s32[]{:S(2)}) async-start(), calls=%async_computation.2 | async-start | bytes 8847360 | tf_op jit(solution)/shard_map/reduce_scatter | solution.py:61
  304.0 66.3 %copy-start.4 = (f32[8,12,4608]{2,0,1:T(8,128)S(1)}, f32[8,12,4608]{2,0,1:T(8,128)}, u32[]{:S(2)}) copy-start(f32[8,12,4608]{2,0,1:T(8,128)} %multiply_add_fusion) | copy-start | bytes 5308420
  304.0 141.3 %all-gather.5.cloned.1.call-start = ((), (), s32[]{:S(2)}) async-start(), calls=%async_computation.3 | async-start | bytes 8847360 | tf_op jit(solution)/shard_map/all_gather | solution.py:65
Sparse Core Ops, SparseCore 0:
  58.8 90.6 all-gather.2
  304.1 66.1 reduce-scatter.1
  373.3 71.9 all-gather.4
where the time goes:
time: 603 us
  blocking collectives  257 us (43%)
  waiting for transfers between devices  229 us (38%)
  matrix products  42 us (7%)
  other arithmetic  35.5 us (6%)
  local copies, waits for them, and re-layouts  17.2 us (3%)
  between operations  13.3 us (2%)
  starting transfers between devices  8.78 us (1%)
    psum x1, blocking collectives, shards(): gram = lax.psum(matmul(projected, projected.T), ('gx', 'gy')) / ncells_all  129 us
    psum x1, blocking collectives, shards(): lax.psum(matmul(prior_flat, phi_all.T), ('gx', 'gy')) / ncells_all  128 us
    all_gather x1, waiting for transfers between devices, shards(): phi_all = lax.all_gather(phi_flat, 'band', axis=0, tiled=True)  79.2 us
    all_gather x1, waiting for transfers between devices, shards(): projected = lax.all_gather(projected_own, 'band', axis=0, tiled=True)  72.1 us
    reduce_scatter x1, waiting for transfers between devices, shards(): lax.psum_scatter(matmul(correlation.T, prior_flat), 'band', scatter_dimen...  66.2 us
    dot_general x4, matrix products, matmul(): jnp.dot(left, right, precision=lax.Precision.HIGHEST, preferred_element_t...  41.8 us
    mul x1, other arithmetic, shards(): phi = -2.0 * lap_flat + potential[None] * block  20.7 us
  transfers between devices with their start and end apart: 7, of which 7 were waited for; matrix products, arithmetic and copies ran while one was open for 2% of the time, Pallas kernels for 0%

commit v1 on v0

--- a/solution.py
+++ b/solution.py
@@ -5,6 +5,12 @@
 
 NZ = 192
 coeffs = (-205.0 / 72.0, 8.0 / 5.0, -1.0 / 5.0, 8.0 / 315.0, -1.0 / 560.0)
+
+
+def summed_here(block, axis):
+    terms = lax.all_gather(block, axis, axis=0, tiled=False)
+    acc = terms.sum(axis=0)
+    return acc
 
 
 def extended_2(x, sides, width):
@@ -63,7 +69,7 @@
     )
     projected_own = phi_flat - removed
     projected = lax.all_gather(projected_own, "band", axis=0, tiled=True)
-    gram = lax.psum(matmul(projected, projected.T), ("gx", "gy")) / ncells_all
+    gram = summed_here(matmul(projected, projected.T), ("gx", "gy")) / ncells_all
     lower = jnp.linalg.cholesky(gram)
     inverse = lax.linalg.triangular_solve(
         lower, jnp.eye(total_count, dtype=lower.dtype), left_side=True, lower=True

time: 603 us -> 519 us (0.86)
  blocking collectives: 257 us -> 172 us
    psum x1 -> x0, blocking collectives: 129 us -> none  [shards(): gram = lax.psum(matmul(projected, projected.T), ('gx', 'gy')) / ncells_all]
    all_gather x0 -> x1, blocking collectives: none -> 44.1 us  [summed_here(): terms = lax.all_gather(block, axis, axis=0, tiled=False)]
where the time goes in v1:
time: 519 us; the launch traced here: 518 us
  waiting for transfers between devices  229 us (44%)
  blocking collectives  172 us (33%)
  matrix products  41.9 us (8%)
  other arithmetic  35.6 us (7%)
  local copies, waits for them, and re-layouts  17.3 us (3%)
  between operations  13.3 us (3%)
  starting transfers between devices  8.78 us (2%)
    psum x1, blocking collectives, shards(): lax.psum(matmul(prior_flat, phi_all.T), ('gx', 'gy')) / ncells_all  128 us
    all_gather x1, waiting for transfers between devices, shards(): phi_all = lax.all_gather(phi_flat, 'band', axis=0, tiled=True)  79.2 us
    all_gather x1, waiting for transfers between devices, shards(): projected = lax.all_gather(projected_own, 'band', axis=0, tiled=True)  72.1 us
    reduce_scatter x1, waiting for transfers between devices, shards(): lax.psum_scatter(matmul(correlation.T, prior_flat), 'band', scatter_dimen...  66.2 us
    all_gather x1, blocking collectives, summed_here(): terms = lax.all_gather(block, axis, axis=0, tiled=False)  44.1 us
    dot_general x4, matrix products, matmul(): jnp.dot(left, right, precision=lax.Precision.HIGHEST, preferred_element_t...  41.7 us
    mul x1, other arithmetic, shards(): phi = -2.0 * lap_flat + potential[None] * block  20.7 us
    reshape x1, local copies, waits for them, and re-layouts, shards(): prior_flat = prior.reshape(prior.shape[0], -1)  11.4 us
  transfers between devices with their start and end apart: 7, of which 7 were waited for; matrix products, arithmetic and copies ran while one was open for 2% of the time, Pallas kernels for 0%

profile of v1, /device:TPU:0, one launch (start us, length us, event | category | flops | bytes accessed | tf_op | source)
XLA Modules:
  0.0 518.5 jit_solution(16955316630726408968)
XLA Ops:
  6.5 0.0 all-gather.4.cloned.1.call-start
  6.5 2.0 reshape.25
  8.5 0.0 copy-start.2
  8.5 0.1 fusion.48
  8.7 1.3 collective-permute-start.1
  10.0 1.3 collective-permute-start
  11.3 0.5 collective-permute-done.1
  11.9 0.1 constant_dynamic-update-slice_fusion.3
  12.0 0.0 copy-done.2
  12.0 0.8 constant_dynamic-update-slice_fusion.1
  12.9 0.0 copy-start.1
  12.9 3.1 collective-permute-done
  16.0 0.1 constant_dynamic-update-slice_fusion
  16.1 0.0 copy-start
  16.1 0.0 copy-start.3
  16.1 0.3 fusion.47
  16.4 0.0 copy-done.1
  16.4 1.3 collective-permute-start.2
  17.7 4.6 collective-permute-start.3
  22.3 6.6 %collective-permute-done.2 = f32[8,20,4,192]{3,2,0,1:T(4,128)S(1)} collective-permute-done((f32[8,20,4,192]{3,2,0,1:T(4,128)S(1)}, f32[8,20,4,192]{3,2,0,1:T(4,128)S(1)}, u32[]{:S(2)}, u32[]{:S(2)}) %collective-permute-start.2) | collective-permute-done | bytes 491552 | tf_op jit(solution)/shard_map/ppermute | solution.py:24
  28.9 1.5 collective-permute-done.3
  30.3 2.9 select_maximum_fusion
  33.2 0.0 copy-done
  33.2 0.0 copy-done.3
  33.2 20.7 %fusion.9 = f32[8,12,24,192]{3,2,0,1:T(8,128)} fusion(f32[8,20,24,192]{3,2,0,1:T(8,128)} %copy-done.3, f32[8,20,4,192]{3,2,0,1:T(4,128)S(1)} %collective-permute-done.3, f32[8,20,4,192]{3,2,0,1:T(4,128)S(1)} %collective-permute-done.2, f32[8,20,32,200]{3,2,0,1:T(8,128)S(1)} %select_maximum_fusion, f32[8,16,24,192]{3,2,0,1:T(8,128)} %copy-done.1, ...), kind=kLoop, calls=%fused_computation.25 | loop fusion | flops 20348928 | bytes 35782656 | tf_op jit(solution)/shard_map/mul | solution.py:62
  53.9 0.0 copy-start.5
  53.9 2.3 mul.78
  56.2 0.0 copy-done.5
  56.2 2.4 multiply_add_fusion
  58.6 0.0 all-gather.4.cloned.1.call-update
  58.7 0.2 reduce-scatter.2.cloned.1.call-start
  58.9 11.4 %copy.10 = f32[12,8,8,4608]{3,2,0,1:T(8,128)} copy(f32[12,8,8,4608]{3,2,1,0:T(8,128)} %bitcast.32) | data formatting | bytes 28311552 | tf_op jit(solution)/shard_map/reshape | solution.py:64
  70.3 79.2 %all-gather.4.cloned.1.call-done = f32[32,55296]{1,0:T(8,128)} async-done(((f32[8,55296]{1,0:T(8,128)}), f32[32,55296]{1,0:T(8,128)}) %all-gather.4.cloned.1.call-update) | async-done | bytes 7077904 | tf_op jit(solution)/shard_map/all_gather | solution.py:65
  149.5 14.5 %convolution_bitcast_fusion = f32[64,32]{0,1:T(8,128)S(1)} fusion(f32[32,55296]{1,0:T(8,128)} %all-gather.4.cloned.1.call-done, f32[64,55296]{1,0:T(8,128)} %bitcast.28), kind=kOutput, calls=%fused_computation.63 | convolution fusion | flops 1358954496 | bytes 21241856 | tf_op jit(solution)/shard_map/dot_general | solution.py:49
  164.0 128.3 %psum.7 = f32[64,32]{0,1:T(8,128)S(1)} all-reduce(f32[64,32]{0,1:T(8,128)S(1)} %convolution_bitcast_fusion), channel_id=1, replica_groups=mesh['gx'=8,'gy'=4,'band'=4] {'gx','gy'}, use_global_device_ids=true, to_apply=%region_0.1 | all-reduce | flops 2048 | bytes 16384 | tf_op jit(solution)/shard_map/psum | solution.py:66
  292.3 11.7 %fusion.40 = f32[32,55296]{1,0:T(8,128)} fusion(f32[64,55296]{1,0:T(8,128)} %bitcast.29, f32[64,32]{0,1:T(8,128)S(1)} %psum.7), kind=kOutput, calls=%fused_computation.78 | convolution fusion | flops 1358956544 | bytes 21241856 | tf_op jit(solution)/shard_map/dot_general | solution.py:49
  304.0 0.0 copy-start.4
  304.0 0.0 reduce-scatter.2.cloned.1.call-update
  304.0 0.0 all-gather.6.cloned.1.call-start
  304.0 66.2 %reduce-scatter.2.cloned.1.call-done = f32[8,55296]{1,0:T(8,128)} async-done(((f32[32,55296]{1,0:T(8,128)}), f32[8,55296]{1,0:T(8,128)}) %reduce-scatter.2.cloned.1.call-update) | async-done | bytes 1769488 | tf_op jit(solution)/shard_map/reduce_scatter | solution.py:67
  370.3 0.0 copy-done.4
  370.3 2.9 sub.3
  373.1 0.0 all-gather.6.cloned.1.call-update
  373.1 72.1 %all-gather.6.cloned.1.call-done = f32[32,55296]{1,0:T(8,128)} async-done(((f32[8,55296]{1,0:T(8,128)}), f32[32,55296]{1,0:T(8,128)}) %all-gather.6.cloned.1.call-update) | async-done | bytes 7077904 | tf_op jit(solution)/shard_map/all_gather | solution.py:71
  445.3 9.0 %fusion.49 = f32[32,32]{1,0:T(8,128)S(1)} fusion(f32[32,55296]{1,0:T(8,128)} %all-gather.6.cloned.1.call-done), kind=kOutput, calls=%fused_computation.91 | convolution fusion | flops 679477248 | bytes 7081984 | tf_op jit(solution)/shard_map/dot_general | solution.py:49
  454.3 44.1 %all-gather = f32[1024,32]{1,0:T(8,128)S(1)} all-gather(f32[32,32]{1,0:T(8,128)S(1)} %fusion.49), channel_id=2, replica_groups=mesh['gx'=8,'gy'=4,'band'=4] {'gx','gy'}, dimensions={0}, use_global_device_ids=true | all-gather | bytes 135168 | tf_op jit(solution)/shard_map/all_gather | solution.py:11
  498.3 0.1 reduce_sum.9
  498.4 0.1 copy.8
  498.5 0.1 copy.9
  498.6 2.9 cholesky.17
  501.5 0.6 compare_reduce_fusion
  502.2 0.7 fusion.36
  502.8 2.4 custom-call.6
  505.3 0.2 fusion.37
  505.5 6.5 %fusion.43 = f32[8,55296]{1,0:T(8,128)} fusion(f32[32,55296]{1,0:T(8,128)} %all-gather.6.cloned.1.call-done, f32[32,32]{1,0:T(8,128)S(1)} %fusion.37, s32[]{:T(128)S(6)} %select_n.8), kind=kOutput, calls=%fused_computation.84 | convolution fusion | flops 169869312 | bytes 8851460 | tf_op jit(solution)/shard_map/dot_general | solution.py:49
  (3 shorter events, 0.0 us)
Async XLA Ops:
  6.5 142.9 %all-gather.4.cloned.1.call-start = ((), (), s32[]{:S(2)}) async-start(), calls=%async_computation.1 | async-start | bytes 8847360 | tf_op jit(solution)/shard_map/all_gather | solution.py:65
  8.5 3.5 copy-start.2
  8.7 3.2 collective-permute-start.1
  10.0 5.9 %collective-permute-start = (f32[8,4,24,192]{3,2,0,1:T(8,128)S(1)}, f32[8,4,24,192]{3,2,0,1:T(8,128)S(1)}, u32[]{:S(2)}, u32[]{:S(2)}) collective-permute-start(f32[8,4,24,192]{3,2,0,1:T(8,128)S(1)} %get-tuple-element.10), channel_id=1, source_target_pairs={{16,0},{32,16},{48,32},{64,48},{80,64},{96,80},{112,96},{17,1},{33... | collective-permute-start | bytes 1769480 | tf_op jit(solution)/shard_map/ppermute | solution.py:24
  12.9 3.5 copy-start.1
  16.1 17.1 %copy-start = (f32[8,16,24,192]{3,2,0,1:T(8,128)}, f32[8,16,24,192]{3,2,0,1:T(8,128)S(1)}, u32[]{:S(2)}) copy-start(f32[8,16,24,192]{3,2,0,1:T(8,128)S(1)} %get-tuple-element.12) | copy-start | bytes 7077892
  16.1 17.1 %copy-start.3 = (f32[8,20,24,192]{3,2,0,1:T(8,128)}, f32[8,20,24,192]{3,2,0,1:T(8,128)S(1)}, u32[]{:S(2)}) copy-start(f32[8,20,24,192]{3,2,0,1:T(8,128)S(1)} %get-tuple-element.13) | copy-start | bytes 8847364
  16.4 12.5 %collective-permute-start.2 = (f32[8,20,4,192]{3,2,0,1:T(4,128)S(1)}, f32[8,20,4,192]{3,2,0,1:T(4,128)S(1)}, u32[]{:S(2)}, u32[]{:S(2)}) collective-permute-start(f32[8,20,4,192]{3,2,0,1:T(4,128)S(1)} %get-tuple-element.5), channel_id=1, source_target_pairs={{4,0},{8,4},{12,8},{5,1},{9,5},{13,9},{6,2},{10,6},{14,10},{7,3},{... | collective-permute-start | bytes 1474568 | tf_op jit(solution)/shard_map/ppermute | solution.py:24
  17.7 12.6 %collective-permute-start.3 = (f32[8,20,4,192]{3,2,0,1:T(4,128)S(1)}, f32[8,20,4,192]{3,2,0,1:T(4,128)S(1)}, u32[]{:S(2)}, u32[]{:S(2)}) collective-permute-start(f32[8,20,4,192]{3,2,0,1:T(4,128)S(1)} %get-tuple-element.6), channel_id=1, source_target_pairs={{0,4},{4,8},{8,12},{1,5},{5,9},{9,13},{2,6},{6,10},{10,14},{3,7},{... | collective-permute-start | bytes 1474568 | tf_op jit(solution)/shard_map/ppermute | solution.py:23
  53.9 2.3 copy-start.5
  58.7 311.6 %reduce-scatter.2.cloned.1.call-start = ((), (), s32[]{:S(2)}) async-start(), calls=%async_computation.2 | async-start | bytes 8847360 | tf_op jit(solution)/shard_map/reduce_scatter | solution.py:67
  304.0 66.3 %copy-start.4 = (f32[8,12,4608]{2,0,1:T(8,128)S(1)}, f32[8,12,4608]{2,0,1:T(8,128)}, u32[]{:S(2)}) copy-start(f32[8,12,4608]{2,0,1:T(8,128)} %multiply_add_fusion) | copy-start | bytes 5308420
  304.0 141.3 %all-gather.6.cloned.1.call-start = ((), (), s32[]{:S(2)}) async-start(), calls=%async_computation.3 | async-start | bytes 8847360 | tf_op jit(solution)/shard_map/all_gather | solution.py:71
Sparse Core Ops, SparseCore 0:
  58.8 90.6 all-gather.3
  304.1 66.1 reduce-scatter.1
  373.3 71.9 all-gather.5
